TPU v7x, 32 devices: a whole 2x2x4 slice. The times are simulated.
32 devices in a mesh: groups: 2 (over y), seg: 4 (over z), ch: 2 (over x), sub: 2 (over core).
Axes of the slice: x: 2, y: 2, z: 4, core: 2. Of those that a mesh axis runs over, the one named last changes fastest.
Arguments:
- rank_series: bfloat16 [2048, 16384], P(('groups', 'ch', 'sub'), 'seg'), parts along dimension 0, may hold values from -6 to 6
- power_series: bfloat16 [2048, 16384], P(('groups', 'ch', 'sub'), 'seg'), parts along dimension 0, may hold values from -6 to 6
- seg_offsets: int32 [32], P(('groups', 'seg')), parts along dimension 0, may hold values from 2048 to 4095, as said below
- bin_index: int32 [128], replicated, may hold values from 0 to 511, as said below
Outputs:
- cross_spectra: bfloat16 [2, 256, 1024, 1024], P(None, ('groups', 'seg'), ('ch', 'sub')), parts along dimension 1
There are 2 independent parts, one for each index of `groups`. A program takes and returns all parts, laid end to end along the dimension named above; an argument that names none is the same for every part. Nothing has to cross between parts.
Inputs may be any that keep to these rules, and one draw needn't show every extreme that they name: `seg_offsets`: every segment reads at least half of its samples past its own 4096 samples, in the following ones. `bin_index`: the bins are distinct.
All inputs are finite; a program needn't handle non-finite values.
Results may differ from a plain program's by a relative error of at most 0.0055.
Values may be sent and summed in bfloat16 or wider, within the bound.
A program may use at most 192 MiB of HBM per device.

v0:
```python
import math
import jax
import jax.numpy as jnp
from jax import lax
from jax.sharding import PartitionSpec as P


def shifted(array, axis, by):
    peers = lax.axis_size(axis)
    pairs = [(i, i + by) for i in range(peers) if 0 <= i + by < peers]
    return lax.ppermute(array, axis, pairs)


def make_kernel(bin_index, length):
    sample_ids = jnp.arange(length, dtype=jnp.int32)
    window = 0.5 - 0.5 * jnp.cos(2.0 * math.pi / length * sample_ids.astype(jnp.float32))
    phase = bin_index[:, None] * sample_ids[None, :] % length
    angle = 2.0 * math.pi / length * phase.astype(jnp.float32)
    factor = (3.0 * length / 8.0) ** (-0.5)
    waves = jnp.stack([jnp.cos(angle), -jnp.sin(angle)]) * factor
    return (waves * window).astype(jnp.bfloat16)


def cut_segments(extended, offsets, length):

    def one_segment(offset):
        return lax.dynamic_slice_in_dim(extended, offset, length, 1)

    return jax.vmap(one_segment)(offsets)


def transform(segments, kernel):
    return jnp.einsum("tkn,scn->stkc", kernel, segments, preferred_element_type=jnp.float32)


def body(rank_series, power_series, seg_offsets, bin_index):
    length = rank_series.shape[1]
    rank_width = rank_series.shape[0]
    series_all = jnp.concatenate([rank_series, power_series], axis=0)
    kernel = make_kernel(bin_index, length)
    next_rim = shifted(series_all, "seg", -1)
    extended = jnp.concatenate([series_all, next_rim], axis=1)
    spectra = transform(cut_segments(extended, seg_offsets, length), kernel)
    spectra = spectra.astype(jnp.bfloat16)
    owned = lax.all_to_all(spectra, "seg", split_axis=2, concat_axis=0, tiled=True)
    rank_owned = owned[..., :rank_width]
    power_owned = owned[..., rank_width:]
    power_piece = lax.all_gather(power_owned, ("ch", "sub"), axis=3, tiled=True)
    swapped = jnp.concatenate([power_piece[:, 1:2], -power_piece[:, 0:1]], axis=1)
    real_part = jnp.einsum(
        "gtkr,gtkp->krp", rank_owned, power_piece, preferred_element_type=jnp.float32
    )
    imag_part = jnp.einsum(
        "gtkr,gtkp->krp", rank_owned, swapped, preferred_element_type=jnp.float32
    )
    return jnp.stack([real_part, imag_part]).astype(jnp.bfloat16)


def solution(mesh):
    return jax.shard_map(
        body,
        mesh=mesh,
        in_specs=(
            P(("groups", "ch", "sub"), "seg"),
            P(("groups", "ch", "sub"), "seg"),
            P(("groups", "seg")),
            P(),
        ),
        out_specs=P(None, ("groups", "seg"), ("ch", "sub"), None),
        check_vma=False,
    )
```

profile of v0, /device:TPU:0, one launch (start us, length us, event | category | flops | bytes accessed | tf_op | source)
XLA Modules:
  0.0 261.1 jit_solution(1151138796967690156)
XLA Ops:
  6.5 3.3 %constant_dynamic-update-slice_fusion.1 = bf16[512,4096]{1,0:T(8,128)(2,1)} fusion(bf16[256,4096]{1,0:T(8,128)(2,1)} %param.4), kind=kLoop, calls=%fused_computation.35 | loop fusion | bytes 4194304
  9.8 1.4 constant_dynamic-update-slice_fusion
  11.3 1.3 collective-permute-start
  12.6 0.1 subtract_multiply_fusion
  12.7 9.7 %fusion.27 = (f32[1,128,4096]{2,1,0:T(8,128)S(1)}, f32[1,128,4096]{2,1,0:T(8,128)}) fusion(s32[128]{0:T(128)S(1)} %copy-done.2), kind=kLoop, calls=%fused_computation.30 | loop fusion | flops 7864320 | bytes 4194816 | tf_op jit(solution)/shard_map/cos | solution.py:20
  22.4 84.7 %collective-permute-done = bf16[512,4096]{1,0:T(8,128)(2,1)} collective-permute-done((bf16[512,4096]{1,0:T(8,128)(2,1)}, bf16[512,4096]{1,0:T(8,128)(2,1)}, u32[]{:S(2)}, u32[]{:S(2)}) %collective-permute-start) | collective-permute-done | bytes 4194336 | tf_op jit(solution)/shard_map/ppermute | solution.py:11
  107.1 7.7 %pad_maximum_fusion.1 = bf16[512,8192]{1,0:T(8,128)(2,1)} fusion(bf16[512,4096]{1,0:T(8,128)(2,1)} %collective-permute-done, bf16[512,4096]{1,0:T(8,128)(2,1)} %constant_dynamic-update-slice_fusion), kind=kLoop, calls=%fused_computation.9 | loop fusion | flops 16777216 | bytes 16777216 | tf_op jit(solution)/shard_map/concatenate | solution.py:42
  114.8 32.7 %while.1 = (s32[]{:T(128)}, bf16[512,8192]{1,0:T(8,128)(2,1)}, s32[4,2]{0,1:T(2,128)S(1)}, bf16[4,512,4096]{2,1,0:T(8,128)(2,1)}, s32[]{:T(128)}) while((s32[]{:T(128)}, bf16[512,8192]{1,0:T(8,128)(2,1)}, s32[4,2]{0,1:T(2,128)S(1)}, bf16[4,512,4096]{2,1,0:T(8,128)(2,1)}, s32[]{:T(128)}) %tuple.18), condition=%wide.while_cond, body=%wide.while_body.sunk | while | flops 2 | bytes 8389221 | solution.py:27
  114.8 0.1 constant_dynamic-slice_fusion.2
  114.8 0.6 slice.38
  115.4 7.5 %bitcast_dynamic-update-slice_fusion.2 = bf16[4,512,4096]{2,1,0:T(8,128)(2,1)} fusion(bf16[4,512,4096]{2,1,0:T(8,128)(2,1)} %get-tuple-element.58, s32[]{:T(128)S(6)} %copy.18, bf16[512,8192]{1,0:T(8,128)(2,1)} %get-tuple-element.61, s32[]{:T(128)} %bitcast.46), kind=kLoop, calls=%fused_computation.clone.1 | loop fusion | bytes 8389124 | tf_op jit(solution)/shard_map/vmap()/gather
  122.9 0.1 constant_dynamic-slice_fusion.2
  123.0 0.6 slice.38
  123.6 7.5 %bitcast_dynamic-update-slice_fusion.2 = bf16[4,512,4096]{2,1,0:T(8,128)(2,1)} fusion(bf16[4,512,4096]{2,1,0:T(8,128)(2,1)} %get-tuple-element.58, s32[]{:T(128)S(6)} %copy.18, bf16[512,8192]{1,0:T(8,128)(2,1)} %get-tuple-element.61, s32[]{:T(128)} %bitcast.46), kind=kLoop, calls=%fused_computation.clone.1 | loop fusion | bytes 8389124 | tf_op jit(solution)/shard_map/vmap()/gather
  131.1 0.1 constant_dynamic-slice_fusion.2
  131.2 0.6 slice.38
  131.8 7.5 %bitcast_dynamic-update-slice_fusion.2 = bf16[4,512,4096]{2,1,0:T(8,128)(2,1)} fusion(bf16[4,512,4096]{2,1,0:T(8,128)(2,1)} %get-tuple-element.58, s32[]{:T(128)S(6)} %copy.18, bf16[512,8192]{1,0:T(8,128)(2,1)} %get-tuple-element.61, s32[]{:T(128)} %bitcast.46), kind=kLoop, calls=%fused_computation.clone.1 | loop fusion | bytes 8389124 | tf_op jit(solution)/shard_map/vmap()/gather
  139.3 0.1 constant_dynamic-slice_fusion.2
  139.4 0.6 slice.38
  139.9 7.5 %bitcast_dynamic-update-slice_fusion.2 = bf16[4,512,4096]{2,1,0:T(8,128)(2,1)} fusion(bf16[4,512,4096]{2,1,0:T(8,128)(2,1)} %get-tuple-element.58, s32[]{:T(128)S(6)} %copy.18, bf16[512,8192]{1,0:T(8,128)(2,1)} %get-tuple-element.61, s32[]{:T(128)} %bitcast.46), kind=kLoop, calls=%fused_computation.clone.1 | loop fusion | bytes 8389124 | tf_op jit(solution)/shard_map/vmap()/gather
  147.5 8.8 %fusion.22 = bf16[4,2,128,512]{2,3,1,0:T(8,128)(2,1)S(1)} fusion(f32[1,128,4096]{2,1,0:T(8,128)} %get-tuple-element.24, f32[1,128,4096]{2,1,0:T(8,128)S(1)} %get-tuple-element.23, f32[4096]{0:T(1024)S(1)} %subtract_multiply_fusion, bf16[4,512,4096]{2,1,0:T(8,128)(2,1)} %get-tuple-element.12), kind=kOutput, calls=%fused_computation.28 | convolution fusion | flops 4298637312 | bytes 22036480 | tf_op jit(solution)/shard_map/tkn,scn->stkc/dot_general | solution.py:33
  156.3 1.0 copy.8
  157.2 28.7 %all_to_all.18 = bf16[4,2,128,512]{3,1,0,2:T(2,128)(2,1)S(1)} all-to-all(bf16[4,2,128,512]{3,1,0,2:T(2,128)(2,1)S(1)} %copy.8), channel_id=1, replica_groups=mesh['groups'=2,'seg'=4,'ch'=2,'sub'=2] {'seg'}, dimensions={2} | all-to-all | bytes 2097152 | tf_op jit(solution)/shard_map/all_to_all | solution.py:45
  185.9 0.3 copy.9
  186.2 0.8 copy.10
  187.1 0.3 all_to_all.16
  187.3 0.8 slice.28
  188.2 22.1 %all-gather.2.cloned.1.call-done = bf16[16,2,32,1024]{3,0,1,2:T(8,128)(2,1)} async-done(((bf16[16,2,32,256]{3,0,1,2:T(8,128)(2,1)}), bf16[16,2,32,1024]{3,0,1,2:T(8,128)(2,1)}) %all-gather.2.cloned.1.call-update) | async-done | bytes 2097168 | tf_op jit(solution)/shard_map/all_gather | solution.py:48
  210.3 3.0 %fusion.33 = (bf16[16,1,32,1024]{3,0,1,2:T(8,128)(2,1)}, bf16[16,1,32,1024]{3,0,1,2:T(8,128)(2,1)}) fusion(bf16[16,2,32,1024]{3,0,1,2:T(8,128)(2,1)} %all-gather.2.cloned.1.call-done), kind=kLoop, calls=%fused_computation.40 | loop fusion | flops 524288 | bytes 4194304 | tf_op jit(solution)/shard_map/slice | solution.py:49
  213.3 9.8 %fusion.1 = bf16[1,32,256,1024]{3,2,1,0:T(8,128)(2,1)} fusion(bf16[16,1,32,1024]{3,0,1,2:T(8,128)(2,1)} %get-tuple-element.22, bf16[16,1,32,1024]{3,0,1,2:T(8,128)(2,1)} %get-tuple-element.21, bf16[16,2,32,512]{3,0,1,2:T(8,128)(2,1)S(1)} %all_to_all.16), kind=kOutput, calls=%fused_computation.6 | convolution fusion | flops 546308096 | bytes 19398656 | tf_op jit(solution)/shard_map/gtkr,gtkp->krp/dot_general | solution.py:53
  223.1 8.1 %fusion = bf16[1,32,256,1024]{3,2,1,0:T(8,128)(2,1)} fusion(bf16[16,2,32,1024]{3,0,1,2:T(8,128)(2,1)S(1)} %copy-done, bf16[16,2,32,512]{3,0,1,2:T(8,128)(2,1)S(1)} %all_to_all.16), kind=kOutput, calls=%fused_computation.5 | convolution fusion | flops 545259520 | bytes 19398656 | tf_op jit(solution)/shard_map/gtkr,gtkp->krp/dot_general | solution.py:50
  231.2 23.0 %pad_maximum_fusion = bf16[2,32,256,1024]{3,2,1,0:T(8,128)(2,1)} fusion(bf16[1,32,256,1024]{3,2,1,0:T(8,128)(2,1)} %fusion.1, bf16[1,32,256,1024]{3,2,1,0:T(8,128)(2,1)} %fusion), kind=kLoop, calls=%fused_computation.2 | loop fusion | flops 16777216 | bytes 67108864 | tf_op jit(solution)/shard_map/stack | solution.py:56
  (13 shorter events, 0.0 us)
Async XLA Ops:
  6.5 3.3 %copy-start.1 = (bf16[256,4096]{1,0:T(8,128)(2,1)S(1)}, bf16[256,4096]{1,0:T(8,128)(2,1)}, u32[]{:S(2)}) copy-start(bf16[256,4096]{1,0:T(8,128)(2,1)} %param.5) | copy-start | bytes 6291460
  6.5 6.0 %copy-start.3 = (s32[4]{0:T(128)S(1)}, s32[4]{0:T(128)}, u32[]{:S(2)}) copy-start(s32[4]{0:T(128)} %param.6) | copy-start | bytes 52
  6.5 6.1 %copy-start.2 = (s32[128]{0:T(128)S(1)}, s32[128]{0:T(128)}, u32[]{:S(2)}) copy-start(s32[128]{0:T(128)} %param.7) | copy-start | bytes 1540
  6.5 203.8 %all-gather.2.cloned.1.call-start = ((), (), s32[]{:S(2)}) async-start(), calls=%async_computation.1 | async-start | bytes 2621440 | tf_op jit(solution)/shard_map/all_gather | solution.py:48
  11.3 95.8 %collective-permute-start = (bf16[512,4096]{1,0:T(8,128)(2,1)}, bf16[512,4096]{1,0:T(8,128)(2,1)}, u32[]{:S(2)}, u32[]{:S(2)}) collective-permute-start(bf16[512,4096]{1,0:T(8,128)(2,1)} %constant_dynamic-update-slice_fusion), channel_id=1, source_target_pairs={{4,0},{8,4},{12,8},{5,1},{9,5},{13,9},{6,2},{10,6},{14,10},{7,3},{... | collective-permute-start | bytes 12582920 | tf_op jit(solution)/shard_map/ppermute | solution.py:11
  213.3 9.8 %copy-start = (bf16[16,2,32,1024]{3,0,1,2:T(8,128)(2,1)S(1)}, bf16[16,2,32,1024]{3,0,1,2:T(8,128)(2,1)}, u32[]{:S(2)}) copy-start(bf16[16,2,32,1024]{3,0,1,2:T(8,128)(2,1)} %all-gather.2.cloned.1.call-done) | copy-start | bytes 6291460
Sparse Core Ops, SparseCore 0:
  188.3 21.9 all-gather.1
where the time goes:
time: 261 us
  waiting for transfers between devices  107 us (41%)
  other arithmetic  43.4 us (17%)
  local copies, waits for them, and re-layouts  40.7 us (16%)
  blocking collectives  28.7 us (11%)
  matrix products  26.7 us (10%)
  between operations  13.5 us (5%)
    ppermute x1, waiting for transfers between devices, shifted(): return lax.ppermute(array, axis, pairs)  84.7 us
    gather x12, local copies, waits for them, and re-layouts  32.7 us
    all_to_all x1, blocking collectives, body(): lax.all_to_all(spectra, 'seg', split_axis=2, concat_axis=0, tiled=True)  28.7 us
    another operation x1, other arithmetic, body(): return jnp.stack([real_part, imag_part]).astype(jnp.bfloat16)  23 us
    all_gather x1, waiting for transfers between devices, body(): power_piece = lax.all_gather(power_owned, ('ch', 'sub'), axis=3, tiled=True)  22.1 us
    dot_general x1, matrix products, body(): jnp.einsum('gtkr,gtkp->krp', rank_owned, swapped, preferred_element_type=...  9.81 us
    cos x1, other arithmetic, make_kernel(): waves = jnp.stack([jnp.cos(angle), -jnp.sin(angle)]) * factor  9.69 us
    dot_general x1, matrix products, transform(): jnp.einsum('tkn,scn->stkc', kernel, segments, preferred_element_type=jnp....  8.77 us
  transfers between devices with their start and end apart: 2, of which 2 were waited for; matrix products, arithmetic and copies ran while one was open for 4% of the time, Pallas kernels for 0%

commit v1 on v0

--- a/solution.py
+++ b/solution.py
@@ -45,7 +45,28 @@
     owned = lax.all_to_all(spectra, "seg", split_axis=2, concat_axis=0, tiled=True)
     rank_owned = owned[..., :rank_width]
     power_owned = owned[..., rank_width:]
-    power_piece = lax.all_gather(power_owned, ("ch", "sub"), axis=3, tiled=True)
+    ways, here, step = (
+        lax.axis_size(("ch", "sub")),
+        lax.axis_index(("ch", "sub")),
+        power_owned.shape[3],
+    )
+    lengths = [n * ways if d == 3 else n for d, n in enumerate(power_owned.shape)]
+    power_piece = lax.dynamic_update_slice_in_dim(
+        jnp.zeros(lengths, power_owned.dtype), power_owned, here * step, axis=3
+    )
+    going_up = going_down = power_owned
+    for far in range(1, ways // 2 + 1):
+        going_up = lax.ppermute(going_up, ("ch", "sub"), [(d, (d + 1) % ways) for d in range(ways)])
+        power_piece = lax.dynamic_update_slice_in_dim(
+            power_piece, going_up, (here - far) % ways * step, axis=3
+        )
+        if 2 * far < ways:
+            going_down = lax.ppermute(
+                going_down, ("ch", "sub"), [(d, (d - 1) % ways) for d in range(ways)]
+            )
+            power_piece = lax.dynamic_update_slice_in_dim(
+                power_piece, going_down, (here + far) % ways * step, axis=3
+            )
     swapped = jnp.concatenate([power_piece[:, 1:2], -power_piece[:, 0:1]], axis=1)
     real_part = jnp.einsum(
         "gtkr,gtkp->krp", rank_owned, power_piece, preferred_element_type=jnp.float32

time: 261 us -> 249 us (0.954)
  blocking collectives: 28.7 us -> 0 us
  waiting for transfers between devices: 107 us -> 127 us
  between operations: 13.5 us -> 0.28 us
  starting transfers between devices: 1.28 us -> 7.04 us
  local copies, waits for them, and re-layouts: 40.7 us -> 45.7 us
    all_to_all x1 -> x0, blocking collectives: 28.7 us -> none  [body(): lax.all_to_all(spectra, 'seg', split_axis=2, concat_axis=0, tiled=True)]
    all_to_all x0 -> x1, waiting for transfers between devices: none -> 24.9 us  [body(): lax.all_to_all(spectra, 'seg', split_axis=2, concat_axis=0, tiled=True)]
    all_gather x1 -> x0, waiting for transfers between devices: 22.1 us -> none  [body(): power_piece = lax.all_gather(power_owned, ('ch', 'sub'), axis=3, tiled=True)]
    ppermute x0 -> x3, waiting for transfers between devices: none -> 17.7 us  [the longest x2 17.7 us: body(): lax.ppermute(going_up, ('ch', 'sub'), [(d, (d + 1) % ways) for d in range...]
    all_to_all x0 -> x1, starting transfers between devices: none -> 4.01 us  [body(): lax.all_to_all(spectra, 'seg', split_axis=2, concat_axis=0, tiled=True)]
    dynamic_update_slice x0 -> x3, local copies, waits for them, and re-layouts: none -> 3.31 us  [the longest x2 2.2 us: body(): lax.dynamic_update_slice_in_dim(power_piece, going_up, (here - far) % way...]
  transfers between devices with their start and end apart: 2 -> 5, of which waited for: 2 -> 4; matrix products, arithmetic and copies ran while one was open for 4% -> 5% of each run, Pallas kernels for 0% -> 0%
where the time goes in v1:
time: 249 us
  waiting for transfers between devices  127 us (51%)
  local copies, waits for them, and re-layouts  45.7 us (18%)
  other arithmetic  41.9 us (17%)
  matrix products  26.5 us (11%)
  starting transfers between devices  7.04 us (3%)
    ppermute x1, waiting for transfers between devices, shifted(): return lax.ppermute(array, axis, pairs)  84.7 us
    gather x12, local copies, waits for them, and re-layouts  33.1 us
    all_to_all x1, waiting for transfers between devices, body(): lax.all_to_all(spectra, 'seg', split_axis=2, concat_axis=0, tiled=True)  24.9 us
    another operation x1, other arithmetic, body(): return jnp.stack([real_part, imag_part]).astype(jnp.bfloat16)  23 us
    ppermute x2, waiting for transfers between devices, body(): lax.ppermute(going_up, ('ch', 'sub'), [(d, (d + 1) % ways) for d in range...  17.7 us
    cos x1, other arithmetic, make_kernel(): waves = jnp.stack([jnp.cos(angle), -jnp.sin(angle)]) * factor  9.7 us
    dot_general x1, matrix products, body(): jnp.einsum('gtkr,gtkp->krp', rank_owned, swapped, preferred_element_type=...  9.63 us
    dot_general x1, matrix products, transform(): jnp.einsum('tkn,scn->stkc', kernel, segments, preferred_element_type=jnp....  8.77 us
  transfers between devices with their start and end apart: 5, of which 4 were waited for; matrix products, arithmetic and copies ran while one was open for 5% of the time, Pallas kernels for 0%

profile of v1, /device:TPU:0, one launch (start us, length us, event | category | flops | bytes accessed | tf_op | source)
XLA Modules:
  0.0 248.7 jit_solution(6503965116900691739)
XLA Ops:
  0.0 3.3 %constant_dynamic-update-slice_fusion.1 = bf16[512,4096]{1,0:T(8,128)(2,1)} fusion(bf16[256,4096]{1,0:T(8,128)(2,1)} %param.4), kind=kLoop, calls=%fused_computation.35 | loop fusion | bytes 4194304
  3.3 1.4 constant_dynamic-update-slice_fusion
  4.7 1.3 collective-permute-start
  6.1 9.7 %fusion.27 = (f32[1,128,4096]{2,1,0:T(8,128)S(1)}, f32[1,128,4096]{2,1,0:T(8,128)}) fusion(s32[128]{0:T(128)S(1)} %copy-done.1), kind=kLoop, calls=%fused_computation.30 | loop fusion | flops 7864320 | bytes 4194816 | tf_op jit(solution)/shard_map/cos | solution.py:20
  15.8 84.7 %collective-permute-done = bf16[512,4096]{1,0:T(8,128)(2,1)} collective-permute-done((bf16[512,4096]{1,0:T(8,128)(2,1)}, bf16[512,4096]{1,0:T(8,128)(2,1)}, u32[]{:S(2)}, u32[]{:S(2)}) %collective-permute-start) | collective-permute-done | bytes 4194336 | tf_op jit(solution)/shard_map/ppermute | solution.py:11
  100.5 7.7 %pad_maximum_fusion.1 = bf16[512,8192]{1,0:T(8,128)(2,1)} fusion(bf16[512,4096]{1,0:T(8,128)(2,1)} %collective-permute-done, bf16[512,4096]{1,0:T(8,128)(2,1)} %constant_dynamic-update-slice_fusion), kind=kLoop, calls=%fused_computation.9 | loop fusion | flops 16777216 | bytes 16777216 | tf_op jit(solution)/shard_map/concatenate | solution.py:42
  108.2 33.1 %while.1 = (s32[]{:T(128)}, bf16[512,8192]{1,0:T(8,128)(2,1)}, s32[4,2]{0,1:T(2,128)S(1)}, bf16[4,512,4096]{2,1,0:T(8,128)(2,1)}, s32[]{:T(128)}) while((s32[]{:T(128)}, bf16[512,8192]{1,0:T(8,128)(2,1)}, s32[4,2]{0,1:T(2,128)S(1)}, bf16[4,512,4096]{2,1,0:T(8,128)(2,1)}, s32[]{:T(128)}) %tuple.19), condition=%wide.while_cond, body=%wide.while_body.sunk | while | flops 2 | bytes 8389221 | solution.py:27
  108.3 0.6 slice.40
  108.9 7.6 %bitcast_dynamic-update-slice_fusion.2 = bf16[4,512,4096]{2,1,0:T(8,128)(2,1)} fusion(bf16[4,512,4096]{2,1,0:T(8,128)(2,1)} %get-tuple-element.60, s32[]{:T(128)S(6)} %copy.18, bf16[512,8192]{1,0:T(8,128)(2,1)} %get-tuple-element.63, s32[]{:T(128)} %bitcast.46), kind=kLoop, calls=%fused_computation.clone.1 | loop fusion | bytes 8389124 | tf_op jit(solution)/shard_map/vmap()/gather
  116.5 0.6 slice.40
  117.1 7.6 %bitcast_dynamic-update-slice_fusion.2 = bf16[4,512,4096]{2,1,0:T(8,128)(2,1)} fusion(bf16[4,512,4096]{2,1,0:T(8,128)(2,1)} %get-tuple-element.60, s32[]{:T(128)S(6)} %copy.18, bf16[512,8192]{1,0:T(8,128)(2,1)} %get-tuple-element.63, s32[]{:T(128)} %bitcast.46), kind=kLoop, calls=%fused_computation.clone.1 | loop fusion | bytes 8389124 | tf_op jit(solution)/shard_map/vmap()/gather
  124.8 0.6 slice.40
  125.4 7.6 %bitcast_dynamic-update-slice_fusion.2 = bf16[4,512,4096]{2,1,0:T(8,128)(2,1)} fusion(bf16[4,512,4096]{2,1,0:T(8,128)(2,1)} %get-tuple-element.60, s32[]{:T(128)S(6)} %copy.18, bf16[512,8192]{1,0:T(8,128)(2,1)} %get-tuple-element.63, s32[]{:T(128)} %bitcast.46), kind=kLoop, calls=%fused_computation.clone.1 | loop fusion | bytes 8389124 | tf_op jit(solution)/shard_map/vmap()/gather
  133.1 0.6 slice.40
  133.7 7.6 %bitcast_dynamic-update-slice_fusion.2 = bf16[4,512,4096]{2,1,0:T(8,128)(2,1)} fusion(bf16[4,512,4096]{2,1,0:T(8,128)(2,1)} %get-tuple-element.60, s32[]{:T(128)S(6)} %copy.18, bf16[512,8192]{1,0:T(8,128)(2,1)} %get-tuple-element.63, s32[]{:T(128)} %bitcast.46), kind=kLoop, calls=%fused_computation.clone.1 | loop fusion | bytes 8389124 | tf_op jit(solution)/shard_map/vmap()/gather
  141.3 8.8 %fusion.22 = bf16[4,2,128,512]{2,3,1,0:T(8,128)(2,1)S(1)} fusion(f32[1,128,4096]{2,1,0:T(8,128)} %get-tuple-element.26, f32[1,128,4096]{2,1,0:T(8,128)S(1)} %get-tuple-element.25, f32[4096]{0:T(1024)S(1)} %subtract_multiply_fusion, bf16[4,512,4096]{2,1,0:T(8,128)(2,1)} %get-tuple-element.12), kind=kOutput, calls=%fused_computation.28 | convolution fusion | flops 4298637312 | bytes 22036480 | tf_op jit(solution)/shard_map/tkn,scn->stkc/dot_general | solution.py:33
  150.1 2.0 copy.8
  152.1 4.0 %all-to-all-start = ((bf16[4,2,128,512]{3,1,0,2:T(2,128)(2,1)}), bf16[4,2,128,512]{3,1,0,2:T(2,128)(2,1)S(1)}, u32[]{:S(2)}, u32[]{:S(2)}) async-start(bf16[4,2,128,512]{3,1,0,2:T(2,128)(2,1)} %copy.8), calls=%async_computation | async-start | bytes 2097152 | tf_op jit(solution)/shard_map/all_to_all | solution.py:45
  156.1 24.9 %all-to-all-done = bf16[4,2,128,512]{3,1,0,2:T(2,128)(2,1)S(1)} async-done(((bf16[4,2,128,512]{3,1,0,2:T(2,128)(2,1)}), bf16[4,2,128,512]{3,1,0,2:T(2,128)(2,1)S(1)}, u32[]{:S(2)}, u32[]{:S(2)}) %all-to-all-start) | async-done | bytes 1048608 | tf_op jit(solution)/shard_map/all_to_all | solution.py:45
  181.0 0.3 copy.9
  181.3 0.8 copy.10
  182.7 0.9 fusion.34
  183.6 1.7 collective-permute-start.2
  185.3 11.0 %collective-permute-done.1 = bf16[16,2,32,256]{3,0,1,2:T(8,128)(2,1)} collective-permute-done((bf16[16,2,32,256]{3,0,1,2:T(8,128)(2,1)}, bf16[16,2,32,256]{3,0,1,2:T(8,128)(2,1)}, u32[]{:S(2)}, u32[]{:S(2)}) %collective-permute-start.1) | collective-permute-done | bytes 524320 | tf_op jit(solution)/shard_map/ppermute | solution.py:59
  196.4 1.1 constant_dynamic-update-slice_fusion.4
  197.5 1.1 constant_dynamic-update-slice_fusion.3
  198.6 6.7 %collective-permute-done.3 = bf16[16,2,32,256]{3,0,1,2:T(8,128)(2,1)} collective-permute-done((bf16[16,2,32,256]{3,0,1,2:T(8,128)(2,1)}, bf16[16,2,32,256]{3,0,1,2:T(8,128)(2,1)}, u32[]{:S(2)}, u32[]{:S(2)}) %collective-permute-start.3) | collective-permute-done | bytes 524320 | tf_op jit(solution)/shard_map/ppermute | solution.py:59
  205.3 1.1 constant_dynamic-update-slice_fusion.2
  206.4 1.5 fusion.33
  207.9 8.1 %fusion = bf16[1,32,256,1024]{3,2,1,0:T(8,128)(2,1)} fusion(bf16[16,2,32,1024]{3,0,1,2:T(8,128)(2,1)S(1)} %constant_dynamic-update-slice_fusion.2, bf16[16,2,32,512]{3,0,1,2:T(8,128)(2,1)S(1)} %all_to_all.16), kind=kOutput, calls=%fused_computation.5 | convolution fusion | flops 545259520 | bytes 19398656 | tf_op jit(solution)/shard_map/gtkr,gtkp->krp/dot_general | solution.py:71
  216.0 9.6 %fusion.1 = bf16[1,32,256,1024]{3,2,1,0:T(8,128)(2,1)} fusion(bf16[16,1,32,1024]{3,0,1,2:T(8,128)(2,1)} %get-tuple-element.22, bf16[16,1,32,1024]{3,0,1,2:T(8,128)(2,1)} %get-tuple-element.21, bf16[16,2,32,512]{3,0,1,2:T(8,128)(2,1)S(1)} %all_to_all.16), kind=kOutput, calls=%fused_computation.6 | convolution fusion | flops 546308096 | bytes 19398656 | tf_op jit(solution)/shard_map/gtkr,gtkp->krp/dot_general | solution.py:74
  225.6 23.0 %pad_maximum_fusion = bf16[2,32,256,1024]{3,2,1,0:T(8,128)(2,1)} fusion(bf16[1,32,256,1024]{3,2,1,0:T(8,128)(2,1)} %fusion.1, bf16[1,32,256,1024]{3,2,1,0:T(8,128)(2,1)} %fusion), kind=kLoop, calls=%fused_computation.2 | loop fusion | flops 16777216 | bytes 67108864 | tf_op jit(solution)/shard_map/stack | solution.py:77
  (19 shorter events, 0.9 us)
Async XLA Ops:
  0.0 3.3 %copy-start = (bf16[256,4096]{1,0:T(8,128)(2,1)S(1)}, bf16[256,4096]{1,0:T(8,128)(2,1)}, u32[]{:S(2)}) copy-start(bf16[256,4096]{1,0:T(8,128)(2,1)} %param.5) | copy-start | bytes 6291460
  3.3 2.7 %copy-start.2 = (s32[4]{0:T(128)S(1)}, s32[4]{0:T(128)}, u32[]{:S(2)}) copy-start(s32[4]{0:T(128)} %param.6) | copy-start | bytes 52
  3.3 2.8 %copy-start.1 = (s32[128]{0:T(128)S(1)}, s32[128]{0:T(128)}, u32[]{:S(2)}) copy-start(s32[128]{0:T(128)} %param.7) | copy-start | bytes 1540
  4.7 95.8 %collective-permute-start = (bf16[512,4096]{1,0:T(8,128)(2,1)}, bf16[512,4096]{1,0:T(8,128)(2,1)}, u32[]{:S(2)}, u32[]{:S(2)}) collective-permute-start(bf16[512,4096]{1,0:T(8,128)(2,1)} %constant_dynamic-update-slice_fusion), channel_id=1, source_target_pairs={{4,0},{8,4},{12,8},{5,1},{9,5},{13,9},{6,2},{10,6},{14,10},{7,3},{... | collective-permute-start | bytes 12582920 | tf_op jit(solution)/shard_map/ppermute | solution.py:11
  152.1 28.9 %all-to-all-start = ((bf16[4,2,128,512]{3,1,0,2:T(2,128)(2,1)}), bf16[4,2,128,512]{3,1,0,2:T(2,128)(2,1)S(1)}, u32[]{:S(2)}, u32[]{:S(2)}) async-start(bf16[4,2,128,512]{3,1,0,2:T(2,128)(2,1)} %copy.8), calls=%async_computation | async-start | bytes 2097152 | tf_op jit(solution)/shard_map/all_to_all | solution.py:45
  183.6 12.8 %collective-permute-start.1 = (bf16[16,2,32,256]{3,0,1,2:T(8,128)(2,1)}, bf16[16,2,32,256]{3,0,1,2:T(8,128)(2,1)}, u32[]{:S(2)}, u32[]{:S(2)}) collective-permute-start(bf16[16,2,32,256]{3,0,1,2:T(8,128)(2,1)} %get-tuple-element.23), channel_id=1, source_target_pairs={{0,1},{1,2},{2,3},{3,0},{4,5},{5,6},{6,7},{7,4},{8,9},{9,10},{10,1... | collective-permute-start | bytes 1572872 | tf_op jit(solution)/shard_map/ppermute | solution.py:59
  183.6 13.9 %collective-permute-start.2 = (bf16[16,2,32,256]{3,0,1,2:T(8,128)(2,1)}, bf16[16,2,32,256]{3,0,1,2:T(8,128)(2,1)}, u32[]{:S(2)}, u32[]{:S(2)}) collective-permute-start(bf16[16,2,32,256]{3,0,1,2:T(8,128)(2,1)} %get-tuple-element.23), channel_id=1, source_target_pairs={{0,3},{1,0},{2,1},{3,2},{4,7},{5,4},{6,5},{7,6},{8,11},{9,8},{10,9... | collective-permute-start | bytes 1572872 | tf_op jit(solution)/shard_map/ppermute | solution.py:64
  196.4 8.9 %collective-permute-start.3 = (bf16[16,2,32,256]{3,0,1,2:T(8,128)(2,1)}, bf16[16,2,32,256]{3,0,1,2:T(8,128)(2,1)}, u32[]{:S(2)}, u32[]{:S(2)}) collective-permute-start(bf16[16,2,32,256]{3,0,1,2:T(8,128)(2,1)} %collective-permute-done.1), channel_id=1, source_target_pairs={{0,1},{1,2},{2,3},{3,0},{4,5},{5,6},{6,7},{7,4},{8,9},{9,10},{10,1... | collective-permute-start | bytes 1572872 | tf_op jit(solution)/shard_map/ppermute | solution.py:59
